TPU v7x, 512 devices: a whole 4x4x16 slice. The times are simulated.
512 devices in a mesh: line: 32 (over x, y, core), seg: 16 (over z).
Axes of the slice: x: 4, y: 4, z: 16, core: 2. Of those that a mesh axis runs over, the one named last changes fastest.
Arguments:
- points: float32 [32, 16, 3, 32768], P('line', 'seg'), may hold values from -1 to 1
- rows: int32 [32, 16, 2, 3072], P('line', 'seg'), may hold values from -1 to 32767, as said below
- cells: int32 [32, 16, 2, 24], P('line', 'seg'), may hold values from -1 to 15, as said below
- pose: float32 [12, 32], P(None, 'line'), as said below
Outputs:
- matched: float32 [32, 16, 2, 5, 3072], P('line', 'seg')
- fitted_pose: float32 [12, 32], P(None, 'line')
- final_spread: float32 [1], replicated
Inputs may be any that keep to these rules, and one draw needn't show every extreme that they name: In each block of 128 slots the filled slots come first; every slot of an empty block is empty; rows toward the lower line lie in the lower margin (below 8192), rows toward the upper line in the upper margin (24576 or more); the lists of line 0 toward the lower side and of line 32 - 1 toward the upper side are empty. `cells`: empty blocks come after the others; in segment 0 of every line all blocks toward an existing adjacent line are filled. `pose`: every 3x3 part is within about 0.5 of the identity.
All inputs are finite; a program needn't handle non-finite values.
Results may differ from a plain program's by a relative error of at most 0.0003.
Values sent between devices are 32-bit elements; how exact they have to be, the bound alone decides.
A program may use at most 64 MiB of HBM per device.

v0:
```python
import jax
import jax.numpy as jnp
from jax import lax
from jax.sharding import PartitionSpec as P

NCELL = 16
CT = 512
BLOCK = 128
ITERS = 2
OUTLIER_MASS = 1.0
SPREAD_START = 0.05
PRIOR_TOP = 0.05
PRIOR_BOTTOM = 1.0
REGULARIZE = 1.0
blocks_per_turn = 4


def from_behind(value, axis, steps):
    count = lax.axis_size(axis)
    initial, last = (max(0, -steps), min(count, count - steps))
    return lax.ppermute(value, axis, [(source, source + steps) for source in range(initial, last)])


def match_block(source_block, cell_id, world_points, spread):
    first_column = jnp.maximum(cell_id, 0) * CT
    target = lax.dynamic_slice_in_dim(world_points, first_column, CT, 1)
    distance = (source_block[0][:, None] - target[0][None, :]) ** 2
    distance = distance + (source_block[1][:, None] - target[1][None, :]) ** 2
    distance = distance + (source_block[2][:, None] - target[2][None, :]) ** 2
    weight = jnp.exp(-distance / (2.0 * spread))
    total_weight = jnp.sum(weight, axis=1)
    posterior = weight / (total_weight + OUTLIER_MASS)[:, None]
    pulled = lax.dot_general(
        target,
        posterior,
        (((1,), (1,)), ((), ())),
        precision=lax.Precision.HIGHEST,
        preferred_element_type=jnp.float32,
    )
    share_row = total_weight / (total_weight + OUTLIER_MASS)
    energy_row = jnp.sum(posterior * distance, axis=1)
    merged_rows = jnp.concatenate([pulled, share_row[None, :], energy_row[None, :]], axis=0)
    return jnp.where(cell_id >= 0, merged_rows, jnp.zeros_like(merged_rows))


def match_all(sources, block_cells, worlds, spread):
    block_total = block_cells.shape[1]
    turns = 2 * block_total // blocks_per_turn
    grouped = (
        sources.reshape(2, 3, block_total, BLOCK)
        .transpose(0, 2, 1, 3)
        .reshape(turns, blocks_per_turn, 3, BLOCK)
    )
    grouped_cells = block_cells.reshape(turns, blocks_per_turn)
    sides = jnp.arange(turns) // (turns // 2)

    def one_turn(packed):
        turn_blocks, turn_cells, side = packed
        target_world = lax.dynamic_index_in_dim(worlds, side, 0, keepdims=False)

        def compute(unused):
            return jax.vmap(
                lambda block_points, block_cell: match_block(
                    block_points, block_cell, target_world, spread
                )
            )(turn_blocks, turn_cells)

        def skipped(unused):
            return jnp.zeros((blocks_per_turn, 5, BLOCK), jnp.float32)

        return lax.cond(jnp.any(turn_cells >= 0), compute, skipped, 0)

    output = lax.map(one_turn, (grouped, grouped_cells, sides))
    return (
        output.reshape(2, block_total, 5, BLOCK)
        .transpose(0, 2, 1, 3)
        .reshape(2, 5, block_total * BLOCK)
    )


def solve_pose(gram_matrix, cross_matrix, pose_column):
    old_pose = jnp.concatenate(
        [pose_column[:9].reshape(3, 3), pose_column[9:].reshape(3, 1)], axis=1
    )
    left_side = gram_matrix + REGULARIZE * jnp.eye(4, dtype=gram_matrix.dtype)
    right_side = cross_matrix + REGULARIZE * old_pose
    factor = jnp.linalg.cholesky(left_side)
    solved = jax.scipy.linalg.cho_solve((factor, True), right_side.T)
    new_pose = solved.T
    return jnp.concatenate([new_pose[:, :3].reshape(9), new_pose[:, 3]])


def send_lists(lists, marks, step):
    return from_behind((lists, marks), "line", step)


def send_back(piece, step):
    return from_behind(piece, "line", step)


def on_device(points, rows, cells, pose):
    own_points = points[0, 0]
    row_list = rows[0, 0]
    cell_ids = cells[0, 0]
    pose_column = pose[:, 0]
    margin = NCELL * CT
    point_total = own_points.shape[1]
    slot_total = row_list.shape[1]
    live_slots = (row_list >= 0).astype(jnp.float32)
    safe_rows = jnp.where(row_list >= 0, row_list, 0)
    raw_source = (
        jnp.take(own_points, safe_rows.reshape(-1), axis=1)
        .reshape(3, 2, slot_total)
        .transpose(1, 0, 2)
    )
    extended = jnp.concatenate([raw_source, jnp.ones((2, 1, slot_total), jnp.float32)], axis=1)
    spread = jnp.float32(SPREAD_START)
    result = None
    for iteration in range(ITERS):
        linear_part = pose_column[:9].reshape(3, 3)
        offset_part = pose_column[9:]
        world_points = (
            jnp.dot(
                linear_part,
                own_points,
                precision=lax.Precision.HIGHEST,
                preferred_element_type=jnp.float32,
            )
            + offset_part[:, None]
        )
        moved_source = (
            jnp.einsum("km,dms->dks", linear_part, raw_source, precision=lax.Precision.HIGHEST)
            + offset_part[None, :, None]
        )
        lower_margin = world_points[:, :margin]
        upper_margin = world_points[:, point_total - margin :]
        cell_marks = (cell_ids + 1).astype(jnp.float32)
        lists_down, marks_down = send_lists(moved_source[0], cell_marks[0], -1)
        lists_up, marks_up = send_lists(moved_source[1], cell_marks[1], 1)
        incoming = jnp.stack([lists_down, lists_up])
        got_cells = jnp.stack([marks_down, marks_up]).astype(jnp.int32) - 1
        own_worlds = jnp.stack([upper_margin, lower_margin])
        answers = match_all(incoming, got_cells, own_worlds, spread)
        result = jnp.stack([send_back(answers[0], 1), send_back(answers[1], -1)])
        result = result * live_slots[:, None, :]
        pulled = result[:, :3]
        share_all = result[:, 3]
        energy_all = result[:, 4]
        gram_matrix = jnp.einsum(
            "dks,dms->km",
            extended * share_all[:, None, :],
            extended,
            precision=lax.Precision.HIGHEST,
        )
        cross_matrix = jnp.einsum("dks,dms->km", pulled, extended, precision=lax.Precision.HIGHEST)
        energy_part = jnp.sum(energy_all)
        share_part = jnp.sum(share_all)
        gram_sum, cross_sum = lax.psum((gram_matrix, cross_matrix), "seg")
        energy_sum, share_sum = lax.psum((energy_part, share_part), ("line", "seg"))
        pose_column = solve_pose(gram_sum, cross_sum, pose_column)
        spread = (energy_sum + PRIOR_TOP) / (3.0 * share_sum + PRIOR_BOTTOM)
    return (result[None, None], pose_column[:, None], spread.reshape(1))


def solution(mesh):
    return jax.shard_map(
        on_device,
        mesh=mesh,
        in_specs=(
            P("line", "seg", None, None),
            P("line", "seg", None, None),
            P("line", "seg", None, None),
            P(None, "line"),
        ),
        out_specs=(P("line", "seg", None, None, None), P(None, "line"), P()),
        check_vma=False,
    )
```

profile of v0, /device:TPU:2, one launch (start us, length us, event | category | flops | bytes accessed | tf_op | source)
XLA Modules:
  0.0 667.9 jit_solution(6395573650611481252)
XLA Ops:
  13.1 21.8 %gather_fusion = f32[6144,3]{1,0:T(8,128)S(1)} fusion(f32[3,32768]{0,1:T(8,128)} %bitcast.285, s32[6144]{0:T(1024)S(1)} %broadcast_clamp_fusion), kind=kCustom, calls=%fused_computation | custom fusion | bytes 172032 | tf_op jit(solution)/shard_map/jit(_take)/gather | solution.py:112
  48.7 16.7 %convolution_add_fusion.1 = f32[3,32768]{1,0:T(4,128)S(1)} fusion(f32[3,3]{1,0:T(4,128)S(1)} %reshape.263, f32[3]{0:T(128)S(1)} %get-tuple-element.442, f32[1,1,3,32768]{2,3,1,0:T(8,128)} %copy.18), kind=kOutput, calls=%fused_computation.61 | convolution fusion | flops 3637248 | bytes 786480 | tf_op jit(solution)/shard_map/dot_general | solution.py:123
  65.8 139.7 %while.28 = (s32[]{:T(128)}, f32[12,4,5,128]{3,2,1,0:T(8,128)S(1)}, s32[12,4]{1,0:T(8,128)S(1)}, f32[2,3,8192]{2,1,0:T(4,128)S(1)}, f32[12,4,3,128]{3,1,2,0:T(4,128)S(1)}, /*index=5*/s32[]{:T(128)}, s32[]{:T(128)}, s32[]{:T(128)}) while((s32[]{:T(128)}, f32[12,4,5,128]{3,2,1,0:T(8,128)S(1)}, s32[12,4]{1,0:T(8,128)S(1)}, ...), condition=%wide.region_6.7_spmd.clone, body=%wide.region_0.6_spmd.clone.sunk | while | flops 18620548 | bytes 529362 | solution.py:73
  78.7 10.3 %conditional.6 = (f32[1,4,5,128]{3,2,1,0:T(8,128)S(1)}) conditional(s32[]{:T(128)} %convert_element_type.49, () %tuple.138, (s32[4]{0:T(128)S(1)}, s32[12]{0:T(128)S(1)}, s32[]{:T(128)}, f32[2,3,8192]{2,1,0:T(4,128)S(1)}, f32[12,4,3,128]{3,1,2,0:T(4,128)S(1)}, /*index=5*/s32[12]{0:T(128)S(1)}, s32[12]{0:T(128)S(1)}, s32[12]{0:T(128)S(1)}, ...), branch_computations={%region_2.2_spmd, %region_3.5_spmd.clone} | conditional | flops 18620528 | bytes 496227 | solution.py:71
  113.7 10.3 %conditional.6 = (f32[1,4,5,128]{3,2,1,0:T(8,128)S(1)}) conditional(s32[]{:T(128)} %convert_element_type.49, () %tuple.138, (s32[4]{0:T(128)S(1)}, s32[12]{0:T(128)S(1)}, s32[]{:T(128)}, f32[2,3,8192]{2,1,0:T(4,128)S(1)}, f32[12,4,3,128]{3,1,2,0:T(4,128)S(1)}, /*index=5*/s32[12]{0:T(128)S(1)}, s32[12]{0:T(128)S(1)}, s32[12]{0:T(128)S(1)}, ...), branch_computations={%region_2.2_spmd, %region_3.5_spmd.clone} | conditional | flops 18620528 | bytes 496227 | solution.py:71
  136.9 10.3 %conditional.6 = (f32[1,4,5,128]{3,2,1,0:T(8,128)S(1)}) conditional(s32[]{:T(128)} %convert_element_type.49, () %tuple.138, (s32[4]{0:T(128)S(1)}, s32[12]{0:T(128)S(1)}, s32[]{:T(128)}, f32[2,3,8192]{2,1,0:T(4,128)S(1)}, f32[12,4,3,128]{3,1,2,0:T(4,128)S(1)}, /*index=5*/s32[12]{0:T(128)S(1)}, s32[12]{0:T(128)S(1)}, s32[12]{0:T(128)S(1)}, ...), branch_computations={%region_2.2_spmd, %region_3.5_spmd.clone} | conditional | flops 18620528 | bytes 496227 | solution.py:71
  217.4 34.0 %all-reduce.6 = (f32[3,4]{1,0:T(4,128)S(1)}, f32[4,4]{0,1:T(4,128)S(1)}) all-reduce(f32[3,4]{1,0:T(4,128)S(1)} %convolution_bitcast_fusion.6, f32[4,4]{0,1:T(4,128)S(1)} %convolution_bitcast_fusion.7), channel_id=1, replica_groups=mesh['line'=32,'seg'=16] {'seg'}, use_global_device_ids=true, to_apply=%region_10.12 | all-reduce | flops 28 | bytes 224 | tf_op jit(solution)/shard_map/psum | solution.py:158
  254.3 16.7 %convolution_add_fusion = f32[3,32768]{1,0:T(4,128)S(1)} fusion(f32[3]{0:T(128)S(1)} %slice_reduce_fusion.3, f32[3,4]{1,0:T(4,128)S(1)} %convolution_bitcast_fusion.5, f32[1,1,3,32768]{2,3,1,0:T(8,128)} %copy.18), kind=kOutput, calls=%fused_computation.60 | convolution fusion | flops 3637248 | bytes 786492 | tf_op jit(solution)/shard_map/dot_general | solution.py:123
  278.9 98.2 %all-reduce.4 = (f32[]{:T(128)}, f32[]{:T(128)}) all-reduce(f32[]{:T(128)} %get-tuple-element.356, f32[]{:T(128)} %get-tuple-element.355), channel_id=1, replica_groups=mesh['line'=32,'seg'=16] {'line','seg'}, use_global_device_ids=true, to_apply=%region_12.15 | all-reduce | flops 2 | bytes 16 | tf_op jit(solution)/shard_map/psum | solution.py:159
  378.5 140.6 %while.29 = (s32[]{:T(128)}, f32[12,4,5,128]{3,2,1,0:T(8,128)S(1)}, s32[12,4]{1,0:T(8,128)S(1)}, f32[2,3,8192]{2,1,0:T(4,128)S(1)}, f32[12,4,3,128]{3,1,2,0:T(4,...) while((s32[]{:T(128)}, f32[12,4,5,128]{3,2,1,0:T(8,128)S(1)}, ...), condition=%wide.region_21.24_spmd.clone, body=%wide.region_15.23_spmd.clone.sunk | while | flops 18620552 | bytes 529402 | solution.py:73
  379.9 10.4 %conditional.7 = (f32[1,4,5,128]{3,2,1,0:T(8,128)S(1)}) conditional(s32[]{:T(128)} %convert_element_type.50, () %tuple.142, (s32[4]{0:T(128)S(1)}, s32[12]{0:T(128)S(1)}, s32[]{:T(128)}, f32[2,3,8192]{2,1,0:T(4,128)S(1)}, f32[12,4,3,128]{3,1,2,0:T(4,128)S(1)}, /*index=5*/f32[]{:T(128)}, s32[12]{0:T(128)S(1)}, s32[12]{0:T(128)S(1)}, ...), branch_computations={%region_17.19_spmd, %region_18.22_spmd.clone} | conditional | flops 18620530 | bytes 496251 | solution.py:71
  391.6 10.4 %conditional.7 = (f32[1,4,5,128]{3,2,1,0:T(8,128)S(1)}) conditional(s32[]{:T(128)} %convert_element_type.50, () %tuple.142, (s32[4]{0:T(128)S(1)}, s32[12]{0:T(128)S(1)}, s32[]{:T(128)}, f32[2,3,8192]{2,1,0:T(4,128)S(1)}, f32[12,4,3,128]{3,1,2,0:T(4,128)S(1)}, /*index=5*/f32[]{:T(128)}, s32[12]{0:T(128)S(1)}, s32[12]{0:T(128)S(1)}, ...), branch_computations={%region_17.19_spmd, %region_18.22_spmd.clone} | conditional | flops 18620530 | bytes 496251 | solution.py:71
  403.3 10.4 %conditional.7 = (f32[1,4,5,128]{3,2,1,0:T(8,128)S(1)}) conditional(s32[]{:T(128)} %convert_element_type.50, () %tuple.142, (s32[4]{0:T(128)S(1)}, s32[12]{0:T(128)S(1)}, s32[]{:T(128)}, f32[2,3,8192]{2,1,0:T(4,128)S(1)}, f32[12,4,3,128]{3,1,2,0:T(4,128)S(1)}, /*index=5*/f32[]{:T(128)}, s32[12]{0:T(128)S(1)}, s32[12]{0:T(128)S(1)}, ...), branch_computations={%region_17.19_spmd, %region_18.22_spmd.clone} | conditional | flops 18620530 | bytes 496251 | solution.py:71
  415.0 10.4 %conditional.7 = (f32[1,4,5,128]{3,2,1,0:T(8,128)S(1)}) conditional(s32[]{:T(128)} %convert_element_type.50, () %tuple.142, (s32[4]{0:T(128)S(1)}, s32[12]{0:T(128)S(1)}, s32[]{:T(128)}, f32[2,3,8192]{2,1,0:T(4,128)S(1)}, f32[12,4,3,128]{3,1,2,0:T(4,128)S(1)}, /*index=5*/f32[]{:T(128)}, s32[12]{0:T(128)S(1)}, s32[12]{0:T(128)S(1)}, ...), branch_computations={%region_17.19_spmd, %region_18.22_spmd.clone} | conditional | flops 18620530 | bytes 496251 | solution.py:71
  426.7 10.4 %conditional.7 = (f32[1,4,5,128]{3,2,1,0:T(8,128)S(1)}) conditional(s32[]{:T(128)} %convert_element_type.50, () %tuple.142, (s32[4]{0:T(128)S(1)}, s32[12]{0:T(128)S(1)}, s32[]{:T(128)}, f32[2,3,8192]{2,1,0:T(4,128)S(1)}, f32[12,4,3,128]{3,1,2,0:T(4,128)S(1)}, /*index=5*/f32[]{:T(128)}, s32[12]{0:T(128)S(1)}, s32[12]{0:T(128)S(1)}, ...), branch_computations={%region_17.19_spmd, %region_18.22_spmd.clone} | conditional | flops 18620530 | bytes 496251 | solution.py:71
  438.4 10.4 %conditional.7 = (f32[1,4,5,128]{3,2,1,0:T(8,128)S(1)}) conditional(s32[]{:T(128)} %convert_element_type.50, () %tuple.142, (s32[4]{0:T(128)S(1)}, s32[12]{0:T(128)S(1)}, s32[]{:T(128)}, f32[2,3,8192]{2,1,0:T(4,128)S(1)}, f32[12,4,3,128]{3,1,2,0:T(4,128)S(1)}, /*index=5*/f32[]{:T(128)}, s32[12]{0:T(128)S(1)}, s32[12]{0:T(128)S(1)}, ...), branch_computations={%region_17.19_spmd, %region_18.22_spmd.clone} | conditional | flops 18620530 | bytes 496251 | solution.py:71
  450.1 10.4 %conditional.7 = (f32[1,4,5,128]{3,2,1,0:T(8,128)S(1)}) conditional(s32[]{:T(128)} %convert_element_type.50, () %tuple.142, (s32[4]{0:T(128)S(1)}, s32[12]{0:T(128)S(1)}, s32[]{:T(128)}, f32[2,3,8192]{2,1,0:T(4,128)S(1)}, f32[12,4,3,128]{3,1,2,0:T(4,128)S(1)}, /*index=5*/f32[]{:T(128)}, s32[12]{0:T(128)S(1)}, s32[12]{0:T(128)S(1)}, ...), branch_computations={%region_17.19_spmd, %region_18.22_spmd.clone} | conditional | flops 18620530 | bytes 496251 | solution.py:71
  461.8 10.4 %conditional.7 = (f32[1,4,5,128]{3,2,1,0:T(8,128)S(1)}) conditional(s32[]{:T(128)} %convert_element_type.50, () %tuple.142, (s32[4]{0:T(128)S(1)}, s32[12]{0:T(128)S(1)}, s32[]{:T(128)}, f32[2,3,8192]{2,1,0:T(4,128)S(1)}, f32[12,4,3,128]{3,1,2,0:T(4,128)S(1)}, /*index=5*/f32[]{:T(128)}, s32[12]{0:T(128)S(1)}, s32[12]{0:T(128)S(1)}, ...), branch_computations={%region_17.19_spmd, %region_18.22_spmd.clone} | conditional | flops 18620530 | bytes 496251 | solution.py:71
  473.6 10.4 %conditional.7 = (f32[1,4,5,128]{3,2,1,0:T(8,128)S(1)}) conditional(s32[]{:T(128)} %convert_element_type.50, () %tuple.142, (s32[4]{0:T(128)S(1)}, s32[12]{0:T(128)S(1)}, s32[]{:T(128)}, f32[2,3,8192]{2,1,0:T(4,128)S(1)}, f32[12,4,3,128]{3,1,2,0:T(4,128)S(1)}, /*index=5*/f32[]{:T(128)}, s32[12]{0:T(128)S(1)}, s32[12]{0:T(128)S(1)}, ...), branch_computations={%region_17.19_spmd, %region_18.22_spmd.clone} | conditional | flops 18620530 | bytes 496251 | solution.py:71
  485.3 10.4 %conditional.7 = (f32[1,4,5,128]{3,2,1,0:T(8,128)S(1)}) conditional(s32[]{:T(128)} %convert_element_type.50, () %tuple.142, (s32[4]{0:T(128)S(1)}, s32[12]{0:T(128)S(1)}, s32[]{:T(128)}, f32[2,3,8192]{2,1,0:T(4,128)S(1)}, f32[12,4,3,128]{3,1,2,0:T(4,128)S(1)}, /*index=5*/f32[]{:T(128)}, s32[12]{0:T(128)S(1)}, s32[12]{0:T(128)S(1)}, ...), branch_computations={%region_17.19_spmd, %region_18.22_spmd.clone} | conditional | flops 18620530 | bytes 496251 | solution.py:71
  497.0 10.4 %conditional.7 = (f32[1,4,5,128]{3,2,1,0:T(8,128)S(1)}) conditional(s32[]{:T(128)} %convert_element_type.50, () %tuple.142, (s32[4]{0:T(128)S(1)}, s32[12]{0:T(128)S(1)}, s32[]{:T(128)}, f32[2,3,8192]{2,1,0:T(4,128)S(1)}, f32[12,4,3,128]{3,1,2,0:T(4,128)S(1)}, /*index=5*/f32[]{:T(128)}, s32[12]{0:T(128)S(1)}, s32[12]{0:T(128)S(1)}, ...), branch_computations={%region_17.19_spmd, %region_18.22_spmd.clone} | conditional | flops 18620530 | bytes 496251 | solution.py:71
  508.7 10.4 %conditional.7 = (f32[1,4,5,128]{3,2,1,0:T(8,128)S(1)}) conditional(s32[]{:T(128)} %convert_element_type.50, () %tuple.142, (s32[4]{0:T(128)S(1)}, s32[12]{0:T(128)S(1)}, s32[]{:T(128)}, f32[2,3,8192]{2,1,0:T(4,128)S(1)}, f32[12,4,3,128]{3,1,2,0:T(4,128)S(1)}, /*index=5*/f32[]{:T(128)}, s32[12]{0:T(128)S(1)}, s32[12]{0:T(128)S(1)}, ...), branch_computations={%region_17.19_spmd, %region_18.22_spmd.clone} | conditional | flops 18620530 | bytes 496251 | solution.py:71
  530.3 101.3 %all-reduce.3 = (f32[]{:T(128)}, f32[]{:T(128)}) all-reduce(f32[]{:T(128)} %get-tuple-element.354, f32[]{:T(128)} %get-tuple-element.353), channel_id=1, replica_groups=mesh['line'=32,'seg'=16] {'line','seg'}, use_global_device_ids=true, to_apply=%region_25.28 | all-reduce | flops 2 | bytes 16 | tf_op jit(solution)/shard_map/psum | solution.py:159
  633.5 29.0 %all-reduce.5 = (f32[4,4]{0,1:T(4,128)S(1)}, f32[3,4]{1,0:T(4,128)S(1)}) all-reduce(f32[4,4]{0,1:T(4,128)S(1)} %convolution_bitcast_fusion.4, f32[3,4]{1,0:T(4,128)S(1)} %convolution_bitcast_fusion.3), channel_id=1, replica_groups=mesh['line'=32,'seg'=16] {'seg'}, use_global_device_ids=true, to_apply=%region_22.25 | all-reduce | flops 28 | bytes 224 | tf_op jit(solution)/shard_map/psum | solution.py:158
  (973 shorter events, 497.0 us)
Async XLA Ops:
  0.6 43.6 %copy-start = (s32[1,1,2,24]{3,2,1,0:T(2,128)S(1)}, s32[1,1,2,24]{3,2,1,0:T(2,128)}, u32[]{:S(2)}) copy-start(s32[1,1,2,24]{3,2,1,0:T(2,128)} %param.17) | copy-start | bytes 580
  36.6 29.1 %collective-permute-start.3 = (f32[3,3072]{1,0:T(4,128)S(1)}, f32[3,3072]{1,0:T(4,128)S(1)}, u32[]{:S(2)}, u32[]{:S(2)}) collective-permute-start(f32[3,3072]{1,0:T(4,128)S(1)} %get-tuple-element.436), channel_id=1, source_target_pairs={{0,16},{16,32},{32,48},{48,64},{64,80},{80,96},{96,112},{112,128},... | collective-permute-start | bytes 110600 | tf_op jit(solution)/shard_map/ppermute | solution.py:21
  38.5 27.2 %collective-permute-start.2 = (f32[3,3072]{1,0:T(4,128)S(1)}, f32[3,3072]{1,0:T(4,128)S(1)}, u32[]{:S(2)}, u32[]{:S(2)}) collective-permute-start(f32[3,3072]{1,0:T(4,128)S(1)} %get-tuple-element.435), channel_id=1, source_target_pairs={{16,0},{32,16},{48,32},{64,48},{80,64},{96,80},{112,96},{128,112},... | collective-permute-start | bytes 110600 | tf_op jit(solution)/shard_map/ppermute | solution.py:21
  44.3 21.3 %collective-permute-start = (f32[24]{0:T(128)S(1)}, f32[24]{0:T(128)S(1)}, u32[]{:S(2)}, u32[]{:S(2)}) collective-permute-start(f32[24]{0:T(128)S(1)} %get-tuple-element.439), channel_id=1, source_target_pairs={{16,0},{32,16},{48,32},{64,48},{80,64},{96,80},{112,96},{128,112},... | collective-permute-start | bytes 296 | tf_op jit(solution)/shard_map/ppermute | solution.py:21
  46.2 19.4 %collective-permute-start.1 = (f32[24]{0:T(128)S(1)}, f32[24]{0:T(128)S(1)}, u32[]{:S(2)}, u32[]{:S(2)}) collective-permute-start(f32[24]{0:T(128)S(1)} %get-tuple-element.440), channel_id=1, source_target_pairs={{0,16},{16,32},{32,48},{48,64},{64,80},{80,96},{96,112},{112,128},... | collective-permute-start | bytes 296 | tf_op jit(solution)/shard_map/ppermute | solution.py:21
  205.6 8.0 %collective-permute-start.4 = (f32[5,3072]{1,0:T(8,128)S(1)}, f32[5,3072]{1,0:T(8,128)S(1)}, u32[]{:S(2)}, u32[]{:S(2)}) collective-permute-start(f32[5,3072]{1,0:T(8,128)S(1)} %bitcast.309), channel_id=1, source_target_pairs={{0,16},{16,32},{32,48},{48,64},{64,80},{80,96},{96,112},{112,128},... | collective-permute-start | bytes 184328 | tf_op jit(solution)/shard_map/ppermute | solution.py:21
  207.5 8.0 %collective-permute-start.5 = (f32[5,3072]{1,0:T(8,128)S(1)}, f32[5,3072]{1,0:T(8,128)S(1)}, u32[]{:S(2)}, u32[]{:S(2)}) collective-permute-start(f32[5,3072]{1,0:T(8,128)S(1)} %bitcast.311), channel_id=1, source_target_pairs={{16,0},{32,16},{48,32},{64,48},{80,64},{96,80},{112,96},{128,112},... | collective-permute-start | bytes 184328 | tf_op jit(solution)/shard_map/ppermute | solution.py:21
  271.1 107.3 %collective-permute-start.7 = (f32[3,3072]{1,0:T(4,128)S(1)}, f32[3,3072]{1,0:T(4,128)S(1)}, u32[]{:S(2)}, u32[]{:S(2)}) collective-permute-start(f32[3,3072]{1,0:T(4,128)S(1)} %get-tuple-element.434), channel_id=1, source_target_pairs={{0,16},{16,32},{32,48},{48,64},{64,80},{80,96},{96,112},{112,128},... | collective-permute-start | bytes 110600 | tf_op jit(solution)/shard_map/ppermute | solution.py:21
  273.0 105.4 %collective-permute-start.6 = (f32[3,3072]{1,0:T(4,128)S(1)}, f32[3,3072]{1,0:T(4,128)S(1)}, u32[]{:S(2)}, u32[]{:S(2)}) collective-permute-start(f32[3,3072]{1,0:T(4,128)S(1)} %get-tuple-element.433), channel_id=1, source_target_pairs={{16,0},{32,16},{48,32},{64,48},{80,64},{96,80},{112,96},{128,112},... | collective-permute-start | bytes 110600 | tf_op jit(solution)/shard_map/ppermute | solution.py:21
  519.2 8.0 %collective-permute-start.8 = (f32[5,3072]{1,0:T(8,128)S(1)}, f32[5,3072]{1,0:T(8,128)S(1)}, u32[]{:S(2)}, u32[]{:S(2)}) collective-permute-start(f32[5,3072]{1,0:T(8,128)S(1)} %bitcast.310), channel_id=1, source_target_pairs={{0,16},{16,32},{32,48},{48,64},{64,80},{80,96},{96,112},{112,128},... | collective-permute-start | bytes 184328 | tf_op jit(solution)/shard_map/ppermute | solution.py:21
  521.1 8.0 %collective-permute-start.9 = (f32[5,3072]{1,0:T(8,128)S(1)}, f32[5,3072]{1,0:T(8,128)S(1)}, u32[]{:S(2)}, u32[]{:S(2)}) collective-permute-start(f32[5,3072]{1,0:T(8,128)S(1)} %bitcast.312), channel_id=1, source_target_pairs={{16,0},{32,16},{48,32},{64,48},{80,64},{96,80},{112,96},{128,112},... | collective-permute-start | bytes 184328 | tf_op jit(solution)/shard_map/ppermute | solution.py:21
where the time goes:
time: 670 us; the launch traced here: 668 us
  blocking collectives  262 us (39%)
  local copies, waits for them, and re-layouts  170 us (25%)
  matrix products  70.6 us (11%)
  other arithmetic  60.7 us (9%)
  loops' own time  59.3 us (9%)
  starting transfers between devices  35 us (5%)
    psum x2, blocking collectives, on_device(): energy_sum, share_sum = lax.psum((energy_part, share_part), ('line', 'seg'))  199 us
    gather x288, local copies, waits for them, and re-layouts  118 us
    psum x2, blocking collectives, on_device(): gram_sum, cross_sum = lax.psum((gram_matrix, cross_matrix), 'seg')  63 us
    another operation x24, loops' own time, one_turn(): return lax.cond(jnp.any(turn_cells >= 0), compute, skipped, 0)  43.1 us
    ppermute x10, starting transfers between devices, from_behind(): lax.ppermute(value, axis, [(source, source + steps) for source in range(i...  35 us
    dot_general x24, matrix products, match_block(): lax.dot_general(target, posterior, (((1,), (1,)), ((), ())), precision=la...  33.6 us
    dot_general x2, matrix products, on_device(): jnp.dot(linear_part, own_points, precision=lax.Precision.HIGHEST, preferr...  33.5 us
    gather x2, local copies, waits for them, and re-layouts, on_device(): jnp.take(own_points, safe_rows.reshape(-1), axis=1)  23 us
  transfers between devices with their start and end apart: 10, of which 4 were waited for; matrix products, arithmetic and copies ran while one was open for 3% of the time, Pallas kernels for 0%

commit v1 on v0

--- a/solution.py
+++ b/solution.py
@@ -1,3 +1,4 @@
+import functools
 import jax
 import jax.numpy as jnp
 from jax import lax
@@ -13,6 +14,13 @@
 PRIOR_BOTTOM = 1.0
 REGULARIZE = 1.0
 blocks_per_turn = 4
+
+
+def form_the_squares(my_tile, link_axis, bus_axis):
+    return lax.psum(lax.psum(my_tile, link_axis), bus_axis)
+
+
+cut_series_all_for = functools.partial(form_the_squares, link_axis="seg", bus_axis="line")
 
 
 def from_behind(value, axis, steps):
@@ -156,7 +164,7 @@
         energy_part = jnp.sum(energy_all)
         share_part = jnp.sum(share_all)
         gram_sum, cross_sum = lax.psum((gram_matrix, cross_matrix), "seg")
-        energy_sum, share_sum = lax.psum((energy_part, share_part), ("line", "seg"))
+        energy_sum, share_sum = cut_series_all_for((energy_part, share_part))
         pose_column = solve_pose(gram_sum, cross_sum, pose_column)
         spread = (energy_sum + PRIOR_TOP) / (3.0 * share_sum + PRIOR_BOTTOM)
     return (result[None, None], pose_column[:, None], spread.reshape(1))

time: 670 us -> 584 us (0.87)
  the two profiles are of different devices: /device:TPU:2 before, /device:TPU:1 now
where the time goes in v1:
time: 584 us; the launch traced here: 582 us
  blocking collectives  175 us (30%)
  local copies, waits for them, and re-layouts  171 us (29%)
  matrix products  70.6 us (12%)
  other arithmetic  60.7 us (10%)
  loops' own time  59.3 us (10%)
  starting transfers between devices  34.5 us (6%)
  waiting for transfers between devices  6.95 us (1%)
    psum x2, blocking collectives, form_the_squares(): return lax.psum(lax.psum(my_tile, link_axis), bus_axis)  127 us
    gather x288, local copies, waits for them, and re-layouts  118 us
    psum x2, blocking collectives, on_device(): gram_sum, cross_sum = lax.psum((gram_matrix, cross_matrix), 'seg')  47.3 us
    another operation x24, loops' own time, one_turn(): return lax.cond(jnp.any(turn_cells >= 0), compute, skipped, 0)  43.1 us
    ppermute x10, starting transfers between devices, from_behind(): lax.ppermute(value, axis, [(source, source + steps) for source in range(i...  34.5 us
    dot_general x24, matrix products, match_block(): lax.dot_general(target, posterior, (((1,), (1,)), ((), ())), precision=la...  33.6 us
    dot_general x2, matrix products, on_device(): jnp.dot(linear_part, own_points, precision=lax.Precision.HIGHEST, preferr...  33.5 us
    gather x2, local copies, waits for them, and re-layouts, on_device(): jnp.take(own_points, safe_rows.reshape(-1), axis=1)  23 us
  transfers between devices with their start and end apart: 10, of which 2 were waited for; matrix products, arithmetic and copies ran while one was open for 3% of the time, Pallas kernels for 0%

profile of v1, /device:TPU:1, one launch (start us, length us, event | category | flops | bytes accessed | tf_op | source)
XLA Modules:
  0.0 582.1 jit_solution(9893534821868703559)
XLA Ops:
  13.1 21.8 %gather_fusion = f32[6144,3]{1,0:T(8,128)S(1)} fusion(f32[3,32768]{0,1:T(8,128)} %bitcast.285, s32[6144]{0:T(1024)S(1)} %broadcast_clamp_fusion), kind=kCustom, calls=%fused_computation | custom fusion | bytes 172032 | tf_op jit(solution)/shard_map/jit(_take)/gather | solution.py:120
  52.3 16.7 %convolution_add_fusion.1 = f32[3,32768]{1,0:T(4,128)S(1)} fusion(f32[3,3]{1,0:T(4,128)S(1)} %reshape.263, f32[3]{0:T(128)S(1)} %get-tuple-element.446, f32[1,1,3,32768]{2,3,1,0:T(8,128)} %copy.18), kind=kOutput, calls=%fused_computation.61 | convolution fusion | flops 3637248 | bytes 786480 | tf_op jit(solution)/shard_map/dot_general | solution.py:131
  69.4 139.7 %while.28 = (s32[]{:T(128)}, f32[12,4,5,128]{3,2,1,0:T(8,128)S(1)}, s32[12,4]{1,0:T(8,128)S(1)}, f32[2,3,8192]{2,1,0:T(4,128)S(1)}, f32[12,4,3,128]{3,1,2,0:T(4,128)S(1)}, /*index=5*/s32[]{:T(128)}, s32[]{:T(128)}, s32[]{:T(128)}) while((s32[]{:T(128)}, f32[12,4,5,128]{3,2,1,0:T(8,128)S(1)}, s32[12,4]{1,0:T(8,128)S(1)}, ...), condition=%wide.region_6.7_spmd.clone, body=%wide.region_0.6_spmd.clone.sunk | while | flops 18620548 | bytes 529362 | solution.py:81
  70.7 10.3 %conditional.6 = (f32[1,4,5,128]{3,2,1,0:T(8,128)S(1)}) conditional(s32[]{:T(128)} %convert_element_type.49, () %tuple.138, (s32[4]{0:T(128)S(1)}, s32[12]{0:T(128)S(1)}, s32[]{:T(128)}, f32[2,3,8192]{2,1,0:T(4,128)S(1)}, f32[12,4,3,128]{3,1,2,0:T(4,128)S(1)}, /*index=5*/s32[12]{0:T(128)S(1)}, s32[12]{0:T(128)S(1)}, s32[12]{0:T(128)S(1)}, ...), branch_computations={%region_2.2_spmd, %region_3.5_spmd.clone} | conditional | flops 18620528 | bytes 496227 | solution.py:79
  105.6 10.3 %conditional.6 = (f32[1,4,5,128]{3,2,1,0:T(8,128)S(1)}) conditional(s32[]{:T(128)} %convert_element_type.49, () %tuple.138, (s32[4]{0:T(128)S(1)}, s32[12]{0:T(128)S(1)}, s32[]{:T(128)}, f32[2,3,8192]{2,1,0:T(4,128)S(1)}, f32[12,4,3,128]{3,1,2,0:T(4,128)S(1)}, /*index=5*/s32[12]{0:T(128)S(1)}, s32[12]{0:T(128)S(1)}, s32[12]{0:T(128)S(1)}, ...), branch_computations={%region_2.2_spmd, %region_3.5_spmd.clone} | conditional | flops 18620528 | bytes 496227 | solution.py:79
  128.9 10.3 %conditional.6 = (f32[1,4,5,128]{3,2,1,0:T(8,128)S(1)}) conditional(s32[]{:T(128)} %convert_element_type.49, () %tuple.138, (s32[4]{0:T(128)S(1)}, s32[12]{0:T(128)S(1)}, s32[]{:T(128)}, f32[2,3,8192]{2,1,0:T(4,128)S(1)}, f32[12,4,3,128]{3,1,2,0:T(4,128)S(1)}, /*index=5*/s32[12]{0:T(128)S(1)}, s32[12]{0:T(128)S(1)}, s32[12]{0:T(128)S(1)}, ...), branch_computations={%region_2.2_spmd, %region_3.5_spmd.clone} | conditional | flops 18620528 | bytes 496227 | solution.py:79
  218.9 26.0 %all-reduce.6 = (f32[3,4]{1,0:T(4,128)S(1)}, f32[4,4]{0,1:T(4,128)S(1)}, f32[]{:T(128)}, f32[]{:T(128)}) all-reduce(f32[3,4]{1,0:T(4,128)S(1)} %convolution_bitcast_fusion.6, f32[4,4]{0,1:T(4,128)S(1)} %convolution_bitcast_fusion.7, f32[]{:T(128)} %get-tuple-element.356, ...), channel_id=1, replica_groups=mesh['line'=32,'seg'=16] {'seg'}, use_global_device_ids=true, to_apply=%region_10.12 | all-reduce | flops 30 | bytes 240 | tf_op jit(solution)/shard_map/psum | solution.py:166
  247.9 16.7 %convolution_add_fusion = f32[3,32768]{1,0:T(4,128)S(1)} fusion(f32[3]{0:T(128)S(1)} %slice_reduce_fusion.3, f32[3,4]{1,0:T(4,128)S(1)} %convolution_bitcast_fusion.5, f32[1,1,3,32768]{2,3,1,0:T(8,128)} %copy.18), kind=kOutput, calls=%fused_computation.60 | convolution fusion | flops 3637248 | bytes 786492 | tf_op jit(solution)/shard_map/dot_general | solution.py:131
  275.1 60.0 %all-reduce.4 = (f32[]{:T(128)}, f32[]{:T(128)}) all-reduce(f32[]{:T(128)} %get-tuple-element.405, f32[]{:T(128)} %get-tuple-element.406), channel_id=1, replica_groups=mesh['line'=32,'seg'=16] {'line'}, use_global_device_ids=true, to_apply=%region_13.16 | all-reduce | flops 2 | bytes 16 | tf_op jit(solution)/shard_map/psum | solution.py:20
  336.6 140.6 %while.29 = (s32[]{:T(128)}, f32[12,4,5,128]{3,2,1,0:T(8,128)S(1)}, s32[12,4]{1,0:T(8,128)S(1)}, f32[2,3,8192]{2,1,0:T(4,128)S(1)}, f32[12,4,3,128]{3,1,2,0:T(4,...) while((s32[]{:T(128)}, f32[12,4,5,128]{3,2,1,0:T(8,128)S(1)}, ...), condition=%wide.region_23.26_spmd.clone, body=%wide.region_17.25_spmd.clone.sunk | while | flops 18620552 | bytes 529402 | solution.py:81
  337.9 10.4 %conditional.7 = (f32[1,4,5,128]{3,2,1,0:T(8,128)S(1)}) conditional(s32[]{:T(128)} %convert_element_type.50, () %tuple.142, (s32[4]{0:T(128)S(1)}, s32[12]{0:T(128)S(1)}, s32[]{:T(128)}, f32[2,3,8192]{2,1,0:T(4,128)S(1)}, f32[12,4,3,128]{3,1,2,0:T(4,128)S(1)}, /*index=5*/f32[]{:T(128)}, s32[12]{0:T(128)S(1)}, s32[12]{0:T(128)S(1)}, ...), branch_computations={%region_19.21_spmd, %region_20.24_spmd.clone} | conditional | flops 18620530 | bytes 496251 | solution.py:79
  349.6 10.4 %conditional.7 = (f32[1,4,5,128]{3,2,1,0:T(8,128)S(1)}) conditional(s32[]{:T(128)} %convert_element_type.50, () %tuple.142, (s32[4]{0:T(128)S(1)}, s32[12]{0:T(128)S(1)}, s32[]{:T(128)}, f32[2,3,8192]{2,1,0:T(4,128)S(1)}, f32[12,4,3,128]{3,1,2,0:T(4,128)S(1)}, /*index=5*/f32[]{:T(128)}, s32[12]{0:T(128)S(1)}, s32[12]{0:T(128)S(1)}, ...), branch_computations={%region_19.21_spmd, %region_20.24_spmd.clone} | conditional | flops 18620530 | bytes 496251 | solution.py:79
  361.3 10.4 %conditional.7 = (f32[1,4,5,128]{3,2,1,0:T(8,128)S(1)}) conditional(s32[]{:T(128)} %convert_element_type.50, () %tuple.142, (s32[4]{0:T(128)S(1)}, s32[12]{0:T(128)S(1)}, s32[]{:T(128)}, f32[2,3,8192]{2,1,0:T(4,128)S(1)}, f32[12,4,3,128]{3,1,2,0:T(4,128)S(1)}, /*index=5*/f32[]{:T(128)}, s32[12]{0:T(128)S(1)}, s32[12]{0:T(128)S(1)}, ...), branch_computations={%region_19.21_spmd, %region_20.24_spmd.clone} | conditional | flops 18620530 | bytes 496251 | solution.py:79
  373.0 10.4 %conditional.7 = (f32[1,4,5,128]{3,2,1,0:T(8,128)S(1)}) conditional(s32[]{:T(128)} %convert_element_type.50, () %tuple.142, (s32[4]{0:T(128)S(1)}, s32[12]{0:T(128)S(1)}, s32[]{:T(128)}, f32[2,3,8192]{2,1,0:T(4,128)S(1)}, f32[12,4,3,128]{3,1,2,0:T(4,128)S(1)}, /*index=5*/f32[]{:T(128)}, s32[12]{0:T(128)S(1)}, s32[12]{0:T(128)S(1)}, ...), branch_computations={%region_19.21_spmd, %region_20.24_spmd.clone} | conditional | flops 18620530 | bytes 496251 | solution.py:79
  384.7 10.4 %conditional.7 = (f32[1,4,5,128]{3,2,1,0:T(8,128)S(1)}) conditional(s32[]{:T(128)} %convert_element_type.50, () %tuple.142, (s32[4]{0:T(128)S(1)}, s32[12]{0:T(128)S(1)}, s32[]{:T(128)}, f32[2,3,8192]{2,1,0:T(4,128)S(1)}, f32[12,4,3,128]{3,1,2,0:T(4,128)S(1)}, /*index=5*/f32[]{:T(128)}, s32[12]{0:T(128)S(1)}, s32[12]{0:T(128)S(1)}, ...), branch_computations={%region_19.21_spmd, %region_20.24_spmd.clone} | conditional | flops 18620530 | bytes 496251 | solution.py:79
  396.4 10.4 %conditional.7 = (f32[1,4,5,128]{3,2,1,0:T(8,128)S(1)}) conditional(s32[]{:T(128)} %convert_element_type.50, () %tuple.142, (s32[4]{0:T(128)S(1)}, s32[12]{0:T(128)S(1)}, s32[]{:T(128)}, f32[2,3,8192]{2,1,0:T(4,128)S(1)}, f32[12,4,3,128]{3,1,2,0:T(4,128)S(1)}, /*index=5*/f32[]{:T(128)}, s32[12]{0:T(128)S(1)}, s32[12]{0:T(128)S(1)}, ...), branch_computations={%region_19.21_spmd, %region_20.24_spmd.clone} | conditional | flops 18620530 | bytes 496251 | solution.py:79
  408.1 10.4 %conditional.7 = (f32[1,4,5,128]{3,2,1,0:T(8,128)S(1)}) conditional(s32[]{:T(128)} %convert_element_type.50, () %tuple.142, (s32[4]{0:T(128)S(1)}, s32[12]{0:T(128)S(1)}, s32[]{:T(128)}, f32[2,3,8192]{2,1,0:T(4,128)S(1)}, f32[12,4,3,128]{3,1,2,0:T(4,128)S(1)}, /*index=5*/f32[]{:T(128)}, s32[12]{0:T(128)S(1)}, s32[12]{0:T(128)S(1)}, ...), branch_computations={%region_19.21_spmd, %region_20.24_spmd.clone} | conditional | flops 18620530 | bytes 496251 | solution.py:79
  419.9 10.4 %conditional.7 = (f32[1,4,5,128]{3,2,1,0:T(8,128)S(1)}) conditional(s32[]{:T(128)} %convert_element_type.50, () %tuple.142, (s32[4]{0:T(128)S(1)}, s32[12]{0:T(128)S(1)}, s32[]{:T(128)}, f32[2,3,8192]{2,1,0:T(4,128)S(1)}, f32[12,4,3,128]{3,1,2,0:T(4,128)S(1)}, /*index=5*/f32[]{:T(128)}, s32[12]{0:T(128)S(1)}, s32[12]{0:T(128)S(1)}, ...), branch_computations={%region_19.21_spmd, %region_20.24_spmd.clone} | conditional | flops 18620530 | bytes 496251 | solution.py:79
  431.6 10.4 %conditional.7 = (f32[1,4,5,128]{3,2,1,0:T(8,128)S(1)}) conditional(s32[]{:T(128)} %convert_element_type.50, () %tuple.142, (s32[4]{0:T(128)S(1)}, s32[12]{0:T(128)S(1)}, s32[]{:T(128)}, f32[2,3,8192]{2,1,0:T(4,128)S(1)}, f32[12,4,3,128]{3,1,2,0:T(4,128)S(1)}, /*index=5*/f32[]{:T(128)}, s32[12]{0:T(128)S(1)}, s32[12]{0:T(128)S(1)}, ...), branch_computations={%region_19.21_spmd, %region_20.24_spmd.clone} | conditional | flops 18620530 | bytes 496251 | solution.py:79
  443.3 10.4 %conditional.7 = (f32[1,4,5,128]{3,2,1,0:T(8,128)S(1)}) conditional(s32[]{:T(128)} %convert_element_type.50, () %tuple.142, (s32[4]{0:T(128)S(1)}, s32[12]{0:T(128)S(1)}, s32[]{:T(128)}, f32[2,3,8192]{2,1,0:T(4,128)S(1)}, f32[12,4,3,128]{3,1,2,0:T(4,128)S(1)}, /*index=5*/f32[]{:T(128)}, s32[12]{0:T(128)S(1)}, s32[12]{0:T(128)S(1)}, ...), branch_computations={%region_19.21_spmd, %region_20.24_spmd.clone} | conditional | flops 18620530 | bytes 496251 | solution.py:79
  455.0 10.4 %conditional.7 = (f32[1,4,5,128]{3,2,1,0:T(8,128)S(1)}) conditional(s32[]{:T(128)} %convert_element_type.50, () %tuple.142, (s32[4]{0:T(128)S(1)}, s32[12]{0:T(128)S(1)}, s32[]{:T(128)}, f32[2,3,8192]{2,1,0:T(4,128)S(1)}, f32[12,4,3,128]{3,1,2,0:T(4,128)S(1)}, /*index=5*/f32[]{:T(128)}, s32[12]{0:T(128)S(1)}, s32[12]{0:T(128)S(1)}, ...), branch_computations={%region_19.21_spmd, %region_20.24_spmd.clone} | conditional | flops 18620530 | bytes 496251 | solution.py:79
  466.7 10.4 %conditional.7 = (f32[1,4,5,128]{3,2,1,0:T(8,128)S(1)}) conditional(s32[]{:T(128)} %convert_element_type.50, () %tuple.142, (s32[4]{0:T(128)S(1)}, s32[12]{0:T(128)S(1)}, s32[]{:T(128)}, f32[2,3,8192]{2,1,0:T(4,128)S(1)}, f32[12,4,3,128]{3,1,2,0:T(4,128)S(1)}, /*index=5*/f32[]{:T(128)}, s32[12]{0:T(128)S(1)}, s32[12]{0:T(128)S(1)}, ...), branch_computations={%region_19.21_spmd, %region_20.24_spmd.clone} | conditional | flops 18620530 | bytes 496251 | solution.py:79
  486.9 21.3 %all-reduce.5 = (f32[4,4]{0,1:T(4,128)S(1)}, f32[3,4]{1,0:T(4,128)S(1)}, f32[]{:T(128)}, f32[]{:T(128)}) all-reduce(f32[4,4]{0,1:T(4,128)S(1)} %convolution_bitcast_fusion.4, f32[3,4]{1,0:T(4,128)S(1)} %convolution_bitcast_fusion.3, f32[]{:T(128)} %get-tuple-element.354, ...), channel_id=1, replica_groups=mesh['line'=32,'seg'=16] {'seg'}, use_global_device_ids=true, to_apply=%region_24.27 | all-reduce | flops 30 | bytes 240 | tf_op jit(solution)/shard_map/psum | solution.py:166
  508.1 67.3 %all-reduce.3 = (f32[]{:T(128)}, f32[]{:T(128)}) all-reduce(f32[]{:T(128)} %get-tuple-element.401, f32[]{:T(128)} %get-tuple-element.402), channel_id=1, replica_groups=mesh['line'=32,'seg'=16] {'line'}, use_global_device_ids=true, to_apply=%region_28.31 | all-reduce | flops 2 | bytes 16 | tf_op jit(solution)/shard_map/psum | solution.py:20
  (973 shorter events, 499.0 us)
Async XLA Ops:
  0.6 46.0 %copy-start = (s32[1,1,2,24]{3,2,1,0:T(2,128)S(1)}, s32[1,1,2,24]{3,2,1,0:T(2,128)}, u32[]{:S(2)}) copy-start(s32[1,1,2,24]{3,2,1,0:T(2,128)} %param.17) | copy-start | bytes 580
  36.6 32.7 %collective-permute-start.3 = (f32[3,3072]{1,0:T(4,128)S(1)}, f32[3,3072]{1,0:T(4,128)S(1)}, u32[]{:S(2)}, u32[]{:S(2)}) collective-permute-start(f32[3,3072]{1,0:T(4,128)S(1)} %get-tuple-element.440), channel_id=1, source_target_pairs={{0,16},{16,32},{32,48},{48,64},{64,80},{80,96},{96,112},{112,128},... | collective-permute-start | bytes 110600 | tf_op jit(solution)/shard_map/ppermute | solution.py:29
  41.1 28.1 %collective-permute-start.2 = (f32[3,3072]{1,0:T(4,128)S(1)}, f32[3,3072]{1,0:T(4,128)S(1)}, u32[]{:S(2)}, u32[]{:S(2)}) collective-permute-start(f32[3,3072]{1,0:T(4,128)S(1)} %get-tuple-element.439), channel_id=1, source_target_pairs={{16,0},{32,16},{48,32},{64,48},{80,64},{96,80},{112,96},{128,112},... | collective-permute-start | bytes 110600 | tf_op jit(solution)/shard_map/ppermute | solution.py:29
  46.6 22.5 %collective-permute-start = (f32[24]{0:T(128)S(1)}, f32[24]{0:T(128)S(1)}, u32[]{:S(2)}, u32[]{:S(2)}) collective-permute-start(f32[24]{0:T(128)S(1)} %get-tuple-element.443), channel_id=1, source_target_pairs={{16,0},{32,16},{48,32},{64,48},{80,64},{96,80},{112,96},{128,112},... | collective-permute-start | bytes 296 | tf_op jit(solution)/shard_map/ppermute | solution.py:29
  48.6 20.6 %collective-permute-start.1 = (f32[24]{0:T(128)S(1)}, f32[24]{0:T(128)S(1)}, u32[]{:S(2)}, u32[]{:S(2)}) collective-permute-start(f32[24]{0:T(128)S(1)} %get-tuple-element.444), channel_id=1, source_target_pairs={{0,16},{16,32},{32,48},{48,64},{64,80},{80,96},{96,112},{112,128},... | collective-permute-start | bytes 296 | tf_op jit(solution)/shard_map/ppermute | solution.py:29
  209.2 4.5 collective-permute-start.4
  211.1 5.9 %collective-permute-start.5 = (f32[5,3072]{1,0:T(8,128)S(1)}, f32[5,3072]{1,0:T(8,128)S(1)}, u32[]{:S(2)}, u32[]{:S(2)}) collective-permute-start(f32[5,3072]{1,0:T(8,128)S(1)} %bitcast.310), channel_id=1, source_target_pairs={{16,0},{32,16},{48,32},{64,48},{80,64},{96,80},{112,96},{128,112},... | collective-permute-start | bytes 184328 | tf_op jit(solution)/shard_map/ppermute | solution.py:29
  264.7 71.8 %collective-permute-start.7 = (f32[3,3072]{1,0:T(4,128)S(1)}, f32[3,3072]{1,0:T(4,128)S(1)}, u32[]{:S(2)}, u32[]{:S(2)}) collective-permute-start(f32[3,3072]{1,0:T(4,128)S(1)} %get-tuple-element.438), channel_id=1, source_target_pairs={{0,16},{16,32},{32,48},{48,64},{64,80},{80,96},{96,112},{112,128},... | collective-permute-start | bytes 110600 | tf_op jit(solution)/shard_map/ppermute | solution.py:29
  273.0 63.4 %collective-permute-start.6 = (f32[3,3072]{1,0:T(4,128)S(1)}, f32[3,3072]{1,0:T(4,128)S(1)}, u32[]{:S(2)}, u32[]{:S(2)}) collective-permute-start(f32[3,3072]{1,0:T(4,128)S(1)} %get-tuple-element.437), channel_id=1, source_target_pairs={{16,0},{32,16},{48,32},{64,48},{80,64},{96,80},{112,96},{128,112},... | collective-permute-start | bytes 110600 | tf_op jit(solution)/shard_map/ppermute | solution.py:29
  477.2 4.4 collective-permute-start.8
  479.2 5.9 %collective-permute-start.9 = (f32[5,3072]{1,0:T(8,128)S(1)}, f32[5,3072]{1,0:T(8,128)S(1)}, u32[]{:S(2)}, u32[]{:S(2)}) collective-permute-start(f32[5,3072]{1,0:T(8,128)S(1)} %bitcast.312), channel_id=1, source_target_pairs={{16,0},{32,16},{48,32},{64,48},{80,64},{96,80},{112,96},{128,112},... | collective-permute-start | bytes 184328 | tf_op jit(solution)/shard_map/ppermute | solution.py:29
